TPU v7x, 32 devices: a whole 2x2x4 slice. The times are simulated.
32 devices in a mesh: trans: 16 (over z, x, core), bin: 2 (over y).
Axes of the slice: x: 2, y: 2, z: 4, core: 2. Of those that a mesh axis runs over, the one named last changes fastest.
Arguments:
- pair_density: bfloat16 [8192, 8000], P('trans', 'bin'), may hold values from -1.5 to 1.5
- bin_index: int32 [8192, 1], P('trans'), may hold values from 0 to 255; in each aligned block of 512 rows (0 to 511, 512 to 1023, ...) at most 4 rows name the same one
- panel_columns: int32 [128], replicated, may hold values from 0 to 7999
Outputs:
- response: float32 [2, 256, 1024000], P(None, None, ('bin', 'trans'))
Inputs may be any that keep to these rules, and one draw needn't show every extreme that they name: `bin_index`: among the 512 transitions of one device no bin occurs more than 4 times, and some bin occurs exactly 4 times. `panel_columns`: entries may repeat.
All inputs are finite; a program needn't handle non-finite values.
Results may differ from a plain program's by a relative error of at most 0.0003.
Values may be sent and summed in bfloat16 or wider, within the bound.
No kernel may reach another device: no remote copies, remote signals or barrier semaphores. Data moves between devices by JAX's collectives and lax.ppermute only.
A program may use at most 256 MiB of HBM per device.

v0:
```python
import jax
import jax.numpy as jnp
from jax import lax
from jax.sharding import PartitionSpec as P

PANEL = 128
NB = 256
MOST = 4
broaden = 1.5


def kernel_tables():
    freq = lax.broadcasted_iota(jnp.int32, (NB,), 0).astype(jnp.float32) + 0.5
    diff = freq[:, None] - freq[None, :]
    total = freq[:, None] + freq[None, :]
    low = diff * diff + broaden * broaden
    high = total * total + broaden * broaden
    return (diff / low - total / high, broaden / high - broaden / low)


def transform(arrived):
    kernel_re, kernel_im = kernel_tables()
    flat = arrived.reshape(arrived.shape[0], arrived.shape[2])
    real_part = jnp.dot(
        kernel_re, flat, precision=lax.Precision.HIGHEST, preferred_element_type=jnp.float32
    )
    imag_part = jnp.dot(
        kernel_im, flat, precision=lax.Precision.HIGHEST, preferred_element_type=jnp.float32
    )
    return jnp.stack([real_part, imag_part])


def local(pair_density, bin_index, panel_columns):
    trans_count = lax.axis_size("trans")
    bin_place = lax.axis_index("bin")
    local_rows, row_count = pair_density.shape
    per_owner = NB // trans_count
    bin_number = bin_index[:, 0]
    matching = bin_number[:, None] == bin_number[None, :]
    earlier = lax.broadcasted_iota(jnp.int32, (local_rows, local_rows), 0) > lax.broadcasted_iota(
        jnp.int32, (local_rows, local_rows), 1
    )
    rank = jnp.sum((matching & earlier).astype(jnp.int32), axis=1)
    slot = bin_number * MOST + rank
    placing = (lax.broadcasted_iota(jnp.int32, (NB * MOST, local_rows), 0) == slot[None, :]).astype(
        jnp.bfloat16
    )
    selector = (
        lax.broadcasted_iota(jnp.int32, (row_count, PANEL), 0) + bin_place * row_count
        == panel_columns[None, :]
    ).astype(jnp.bfloat16)
    send_rows = jnp.dot(placing, pair_density, preferred_element_type=jnp.float32).astype(
        jnp.bfloat16
    )
    got_rows = lax.all_to_all(send_rows, "trans", split_axis=0, concat_axis=0, tiled=True)
    got_panel = lax.psum(
        jnp.dot(got_rows, selector, preferred_element_type=jnp.float32).astype(jnp.bfloat16), "bin"
    )
    rows_split = got_rows.reshape(trans_count, per_owner, MOST, row_count)
    panel_split = got_panel.reshape(trans_count, per_owner, MOST, PANEL)
    spectral = jnp.einsum(
        "sbmg,sbmc->bgc", rows_split, panel_split, preferred_element_type=jnp.float32
    )
    piece_width = row_count * PANEL // trans_count
    slab = spectral.reshape(per_owner, trans_count, piece_width)
    arrived = lax.all_to_all(slab, "trans", split_axis=1, concat_axis=0, tiled=True)
    response = transform(arrived)
    return response


def solution(mesh):
    placed = (P("trans", "bin"), P("trans", None), P())
    return jax.shard_map(
        local,
        mesh=mesh,
        in_specs=placed,
        out_specs=P(None, None, ("bin", "trans")),
        check_vma=False,
    )
```

profile of v0, /device:TPU:11, one launch (start us, length us, event | category | flops | bytes accessed | tf_op | source)
XLA Modules:
  0.0 1157.1 jit_solution(17632754684267863969)
XLA Ops:
  6.5 0.0 copy-start
  6.5 1.0 convert_reduce_fusion
  7.5 0.7 multiply_add_fusion
  8.2 8.9 convolution_convert_fusion
  17.1 11.7 %copy.10 = bf16[1024,4000]{1,0:T(8,128)(2,1)} copy(bf16[1024,4000]{0,1:T(8,128)(2,1)} %convolution_convert_fusion) | data formatting | bytes 16384000 | tf_op jit(solution)/shard_map/convert_element_type | solution.py:52
  28.8 6.5 all-to-all-start
  35.4 0.2 all-reduce.2.cloned.1.call-start
  35.6 182.1 %all-to-all-done = bf16[16,64,4000]{2,1,0:T(8,128)(2,1)} async-done(((bf16[16,64,4000]{2,1,0:T(8,128)(2,1)}), bf16[16,64,4000]{2,1,0:T(8,128)(2,1)}, u32[]{:S(2)}, u32[]{:S(2)}) %all-to-all-start) | async-done | bytes 8192032 | tf_op jit(solution)/shard_map/all_to_all | solution.py:55
  217.7 0.0 copy-done
  217.7 5.8 fusion.2
  223.5 0.9 copy.12
  224.4 0.0 all-reduce.2.cloned.1.call-update
  224.4 11.2 copy.11
  235.6 11.2 all-reduce.2.cloned.1.call-done
  246.8 16.1 %convolution_bitcast_fusion.2 = f32[16,4000,128]{2,1,0:T(8,128)} fusion(bf16[16,16,4,4000]{3,0,2,1:T(8,128)(2,1)} %bitcast.24, bf16[16,16,4,128]{3,0,2,1:T(8,128)(2,1)} %all-reduce.2.cloned.1.call-done), kind=kOutput, calls=%fused_computation.3 | convolution fusion | flops 1048576000 | bytes 41222144 | tf_op jit(solution)/shard_map/sbmg,sbmc->bgc/dot_general | solution.py:61
  263.0 29.6 %reshape.38 = f32[16,16,32000]{2,1,0:T(8,128)} reshape(f32[16,4000,128]{2,1,0:T(8,128)} %convolution_bitcast_fusion.2) | data formatting | bytes 65536000 | tf_op jit(solution)/shard_map/reshape | solution.py:65
  292.6 27.4 %copy.13 = f32[16,16,32000]{2,0,1:T(8,128)} copy(f32[16,16,32000]{2,1,0:T(8,128)} %reshape.38) | data formatting | bytes 65536000 | tf_op jit(solution)/shard_map/reshape | solution.py:65
  320.0 7.2 all-to-all-start.1
  327.3 704.8 %all-to-all-done.1 = f32[16,16,32000]{2,0,1:T(8,128)} async-done(((f32[16,16,32000]{2,0,1:T(8,128)}), f32[16,16,32000]{2,0,1:T(8,128)}, u32[]{:S(2)}, u32[]{:S(2)}) %all-to-all-start.1) | async-done | bytes 32768032 | tf_op jit(solution)/shard_map/all_to_all | solution.py:66
  1032.1 37.1 %convolution_bitcast_fusion = f32[1,256,32000]{2,1,0:T(8,128)} fusion(f32[256,32000]{1,0:T(8,128)} %bitcast.9, f32[256]{0:T(256)S(1)} %convert_add_fusion), kind=kOutput, calls=%fused_computation.1 | convolution fusion | flops 25166413824 | bytes 65537024 | tf_op jit(solution)/shard_map/dot_general | solution.py:27
  1069.1 37.1 %convolution_bitcast_fusion.1 = f32[1,256,32000]{2,1,0:T(8,128)} fusion(f32[256,32000]{1,0:T(8,128)} %bitcast.9, f32[256]{0:T(256)S(1)} %convert_add_fusion), kind=kOutput, calls=%fused_computation.2 | convolution fusion | flops 25166413824 | bytes 65537024 | tf_op jit(solution)/shard_map/dot_general | solution.py:24
  1106.3 43.9 %pad_maximum_fusion = f32[2,256,32000]{2,1,0:T(8,128)} fusion(f32[1,256,32000]{2,1,0:T(8,128)} %convolution_bitcast_fusion, f32[1,256,32000]{2,1,0:T(8,128)} %convolution_bitcast_fusion.1), kind=kLoop, calls=%fused_computation | loop fusion | flops 16384000 | bytes 131072000 | tf_op jit(solution)/shard_map/stack | solution.py:30
  (2 shorter events, 0.0 us)
Async XLA Ops:
  6.5 211.2 %copy-start = (s32[128]{0:T(128)S(1)}, s32[128]{0:T(128)}, u32[]{:S(2)}) copy-start(s32[128]{0:T(128)} %param.5) | copy-start | bytes 1540
  28.8 188.9 %all-to-all-start = ((bf16[16,64,4000]{2,1,0:T(8,128)(2,1)}), bf16[16,64,4000]{2,1,0:T(8,128)(2,1)}, u32[]{:S(2)}, u32[]{:S(2)}) async-start(bf16[16,64,4000]{2,1,0:T(8,128)(2,1)} %bitcast.23), calls=%async_computation | async-start | bytes 16777216 | tf_op jit(solution)/shard_map/all_to_all | solution.py:55
  35.4 211.4 %all-reduce.2.cloned.1.call-start = ((), (), s32[]{:S(2)}) async-start(), calls=%async_computation.2 | async-start | bytes 524288 | tf_op jit(solution)/shard_map/psum | solution.py:56
  320.0 712.0 %all-to-all-start.1 = ((f32[16,16,32000]{2,0,1:T(8,128)}), f32[16,16,32000]{2,0,1:T(8,128)}, u32[]{:S(2)}, u32[]{:S(2)}) async-start(f32[16,16,32000]{2,0,1:T(8,128)} %copy.13), calls=%async_computation.1 | async-start | bytes 65536000 | tf_op jit(solution)/shard_map/all_to_all | solution.py:66
Sparse Core Ops, SparseCore 0:
  224.6 22.2 all-reduce.1
where the time goes:
time: 1160 us
  waiting for transfers between devices  898 us (77%)
  matrix products  105 us (9%)
  local copies, waits for them, and re-layouts  80.8 us (7%)
  other arithmetic  45.6 us (4%)
  starting transfers between devices  14 us (1%)
  between operations  13.4 us (1%)
    all_to_all x1, waiting for transfers between devices, local(): lax.all_to_all(slab, 'trans', split_axis=1, concat_axis=0, tiled=True)  705 us
    all_to_all x1, waiting for transfers between devices, local(): lax.all_to_all(send_rows, 'trans', split_axis=0, concat_axis=0, tiled=True)  182 us
    reshape x2, local copies, waits for them, and re-layouts, local(): slab = spectral.reshape(per_owner, trans_count, piece_width)  57.1 us
    another operation x1, other arithmetic, transform(): return jnp.stack([real_part, imag_part])  43.9 us
    dot_general x1, matrix products, transform(): jnp.dot(kernel_re, flat, precision=lax.Precision.HIGHEST, preferred_eleme...  37.1 us
    dot_general x1, matrix products, transform(): jnp.dot(kernel_im, flat, precision=lax.Precision.HIGHEST, preferred_eleme...  37.1 us
  transfers between devices with their start and end apart: 3, of which 3 were waited for; matrix products, arithmetic and copies ran while one was open for 1% of the time, Pallas kernels for 0%

commit v1 on v0

--- a/solution.py
+++ b/solution.py
@@ -63,7 +63,10 @@
     )
     piece_width = row_count * PANEL // trans_count
     slab = spectral.reshape(per_owner, trans_count, piece_width)
-    arrived = lax.all_to_all(slab, "trans", split_axis=1, concat_axis=0, tiled=True)
+    arrived = jnp.concatenate(
+        lax.all_to_all(jnp.stack(jnp.split(slab, lax.axis_size("trans"), axis=1)), "trans", 0, 0),
+        axis=0,
+    )
     response = transform(arrived)
     return response
 

time: 1160 us -> 1300 us (1.12)
  local copies, waits for them, and re-layouts: 80.8 us -> 217 us
    unnamed x2 -> x18, local copies, waits for them, and re-layouts: 0.01 us -> 155 us
    reshape x2 -> x1, local copies, waits for them, and re-layouts: 57.1 us -> 30 us  [local(): slab = spectral.reshape(per_owner, trans_count, piece_width)]
where the time goes in v1:
time: 1300 us; the launch traced here: 1290 us
  waiting for transfers between devices  898 us (69%)
  local copies, waits for them, and re-layouts  217 us (17%)
  matrix products  105 us (8%)
  other arithmetic  45.6 us (4%)
  between operations  13.9 us (1%)
  starting transfers between devices  13.8 us (1%)
    all_to_all x1, waiting for transfers between devices, local(): lax.all_to_all(jnp.stack(jnp.split(slab, lax.axis_size('trans'), axis=1))...  705 us
    all_to_all x1, waiting for transfers between devices, local(): lax.all_to_all(send_rows, 'trans', split_axis=0, concat_axis=0, tiled=True)  182 us
    unnamed x18, local copies, waits for them, and re-layouts  155 us
    another operation x1, other arithmetic, transform(): return jnp.stack([real_part, imag_part])  43.9 us
    dot_general x1, matrix products, transform(): jnp.dot(kernel_re, flat, precision=lax.Precision.HIGHEST, preferred_eleme...  37.3 us
    dot_general x1, matrix products, transform(): jnp.dot(kernel_im, flat, precision=lax.Precision.HIGHEST, preferred_eleme...  37 us
    reshape x1, local copies, waits for them, and re-layouts, local(): slab = spectral.reshape(per_owner, trans_count, piece_width)  30 us
  transfers between devices with their start and end apart: 3, of which 3 were waited for; matrix products, arithmetic and copies ran while one was open for 1% of the time, Pallas kernels for 0%

profile of v1, /device:TPU:11, one launch (start us, length us, event | category | flops | bytes accessed | tf_op | source)
XLA Modules:
  0.0 1293.7 jit_solution(4786889394883764445)
XLA Ops:
  8.2 8.9 convolution_convert_fusion
  17.2 11.7 copy.9
  35.6 182.1 %all-to-all-done = bf16[16,64,4000]{2,1,0:T(8,128)(2,1)} async-done(((bf16[16,64,4000]{2,1,0:T(8,128)(2,1)}), bf16[16,64,4000]{2,1,0:T(8,128)(2,1)}, u32[]{:S(2)}, u32[]{:S(2)}) %all-to-all-start) | async-done | bytes 8192032 | tf_op jit(solution)/shard_map/all_to_all | solution.py:55
  224.4 11.2 copy.10
  235.6 11.2 all-reduce.2.cloned.1.call-done
  246.8 16.1 %convolution_bitcast_fusion.2 = f32[16,4000,128]{2,1,0:T(8,128)} fusion(bf16[16,16,4,4000]{3,0,2,1:T(8,128)(2,1)} %bitcast.86, bf16[16,16,4,128]{3,0,2,1:T(8,128)(2,1)} %all-reduce.2.cloned.1.call-done), kind=kOutput, calls=%fused_computation.3 | convolution fusion | flops 1048576000 | bytes 41222144 | tf_op jit(solution)/shard_map/sbmg,sbmc->bgc/dot_general | solution.py:61
  263.0 30.0 %reshape.34 = f32[16,16,32000]{2,1,0:T(8,128)} reshape(f32[16,4000,128]{2,1,0:T(8,128)} %convolution_bitcast_fusion.2) | data formatting | bytes 65536000 | tf_op jit(solution)/shard_map/reshape | solution.py:65
  301.0 8.7 fusion.14
  309.7 8.7 fusion.13
  318.4 8.7 fusion.12
  327.1 8.7 fusion.11
  335.9 8.7 fusion.10
  344.6 8.9 fusion.9
  353.4 8.7 fusion.8
  370.2 8.7 fusion.6
  378.9 8.7 fusion.5
  396.3 8.7 fusion.3
  405.0 8.9 fusion.2
  413.9 8.7 fusion.1
  438.4 704.8 %all-to-all-done.1 = f32[16,16,1,32000]{3,2,1,0:T(1,128)} async-done(((f32[16,16,1,32000]{3,2,1,0:T(1,128)}), f32[16,16,1,32000]{3,2,1,0:T(1,128)}, u32[]{:S(2)}, u32[]{:S(2)}) %all-to-all-start.1) | async-done | bytes 32768032 | tf_op jit(solution)/shard_map/all_to_all | solution.py:67
  1143.2 25.0 %copy.13 = f32[16,16,1,32000]{3,1,2,0:T(8,128)} copy(f32[16,16,1,32000]{3,2,1,0:T(1,128)} %all-to-all-done.1) | data formatting | bytes 65536000
  1168.1 37.0 %convolution_bitcast_fusion = f32[1,256,32000]{2,1,0:T(8,128)} fusion(f32[256,32000]{1,0:T(8,128)} %bitcast.83, f32[256]{0:T(256)S(1)} %convert_add_fusion), kind=kOutput, calls=%fused_computation.1 | convolution fusion | flops 25166413824 | bytes 65537024 | tf_op jit(solution)/shard_map/dot_general | solution.py:27
  1205.2 37.3 %convolution_bitcast_fusion.1 = f32[1,256,32000]{2,1,0:T(8,128)} fusion(f32[256,32000]{1,0:T(8,128)} %bitcast.84, f32[256]{0:T(256)S(1)} %convert_add_fusion), kind=kOutput, calls=%fused_computation.2 | convolution fusion | flops 25166413824 | bytes 65537024 | tf_op jit(solution)/shard_map/dot_general | solution.py:24
  1242.5 43.9 %pad_maximum_fusion = f32[2,256,32000]{2,1,0:T(8,128)} fusion(f32[1,256,32000]{2,1,0:T(8,128)} %convolution_bitcast_fusion, f32[1,256,32000]{2,1,0:T(8,128)} %convolution_bitcast_fusion.1), kind=kLoop, calls=%fused_computation | loop fusion | flops 16384000 | bytes 131072000 | tf_op jit(solution)/shard_map/stack | solution.py:30
  (16 shorter events, 55.6 us)
Async XLA Ops:
  6.5 211.2 %copy-start = (s32[128]{0:T(128)S(1)}, s32[128]{0:T(128)}, u32[]{:S(2)}) copy-start(s32[128]{0:T(128)} %param.5) | copy-start | bytes 1540
  28.9 188.9 %all-to-all-start = ((bf16[16,64,4000]{2,1,0:T(8,128)(2,1)}), bf16[16,64,4000]{2,1,0:T(8,128)(2,1)}, u32[]{:S(2)}, u32[]{:S(2)}) async-start(bf16[16,64,4000]{2,1,0:T(8,128)(2,1)} %bitcast.85), calls=%async_computation | async-start | bytes 16777216 | tf_op jit(solution)/shard_map/all_to_all | solution.py:55
  35.4 211.5 %all-reduce.2.cloned.1.call-start = ((), (), s32[]{:S(2)}) async-start(), calls=%async_computation.2 | async-start | bytes 524288 | tf_op jit(solution)/shard_map/psum | solution.py:56
  431.4 711.8 %all-to-all-start.1 = ((f32[16,16,1,32000]{3,2,1,0:T(1,128)}), f32[16,16,1,32000]{3,2,1,0:T(1,128)}, u32[]{:S(2)}, u32[]{:S(2)}) async-start(f32[16,16,1,32000]{3,2,1,0:T(1,128)} %fusion), calls=%async_computation.1 | async-start | bytes 65536000 | tf_op jit(solution)/shard_map/all_to_all | solution.py:67
Sparse Core Ops, SparseCore 0:
  224.6 22.2 all-reduce.1
